TPU v7x, 128 devices: a whole 4x4x4 slice. The times are simulated.
128 devices in a mesh: ctx: 16 (over y, x_hi, core), tp: 8 (over x_lo, z).
Axes of the slice: x: 4 (x_hi: 2, x_lo: 2; x = x_hi * 2 + x_lo), y: 4, z: 4, core: 2. Of those that a mesh axis runs over, the one named last changes fastest.
Arguments:
- hyena_query: bfloat16 [6144, 8192], P('ctx', 'tp'), may hold values from -6 to 6
- hyena_key: bfloat16 [6144, 8192], P('ctx', 'tp'), may hold values from -6 to 6
- hyena_value: bfloat16 [6144, 8192], P('ctx', 'tp'), may hold values from -6 to 6
- conv_filter: bfloat16 [512, 128], P('tp'), may hold values from -0.5 to 0.5
- skip_gain: float32 [8192], P('tp'), may hold values from -4 to 4
- query_rows: bfloat16 [6144, 8192], P('ctx', 'tp'), may hold values from -80 to 80
- key_rows: bfloat16 [6144, 8192], P('ctx', 'tp'), may hold values from -4 to 4, as said below
- value_rows: bfloat16 [6144, 8192], P('ctx', 'tp'), may hold values from -6 to 6
- out_weight: bfloat16 [8192, 8192], P(None, 'tp'), may hold values from -1 to 1
Outputs:
- hyena_out: bfloat16 [6144, 8192], P('ctx', 'tp')
- attention_out: bfloat16 [8192, 6144], P('tp', 'ctx')
Inputs may be any that keep to these rules, and one draw needn't show every extreme that they name: `key_rows`: keys of order one.
All inputs are finite; a program needn't handle non-finite values.
Results may differ from a plain program's by a relative error of at most 0.014.
Values may be sent and summed in bfloat16 or wider, within the bound.
No kernel may reach another device: no remote copies, remote signals or barrier semaphores. Data moves between devices by JAX's collectives and lax.ppermute only.
A program may use at most 128 MiB of HBM per device.

v0:
```python
import jax
import jax.numpy as jnp
from jax import lax
from jax.sharding import PartitionSpec as P

HEAD_DIM = 128


def shifted(block, axis, distance):
    devices = range(lax.axis_size(axis))
    route = [(i - distance, i) for i in devices if i - distance in devices]
    return lax.ppermute(block, axis, route)


def toeplitz_pair(filters):
    length = filters.shape[1]
    lag_table = (
        jnp.arange(length, dtype=jnp.int32)[:, None] - jnp.arange(length, dtype=jnp.int32)[None, :]
    )
    taps = jnp.arange(length, dtype=jnp.int32)[:, None, None]
    inner_table = (lag_table[None] == taps).astype(jnp.bfloat16)
    outer_table = (lag_table[None] + length == taps).astype(jnp.bfloat16)
    inner_part = jnp.einsum(
        "gj,jts->gts", filters, inner_table, preferred_element_type=jnp.float32
    ).astype(jnp.bfloat16)
    outer_part = jnp.einsum(
        "gj,jts->gts", filters, outer_table, preferred_element_type=jnp.float32
    ).astype(jnp.bfloat16)
    return (inner_part, outer_part)


def local_conv(current, before, filters):
    blocks, length, feature_width = current.shape
    groups = filters.shape[0]
    split_shape = (blocks, length, groups, feature_width // groups)
    inner_part, outer_part = toeplitz_pair(filters)
    result = jnp.einsum(
        "gts,bsgc->btgc",
        inner_part,
        current.reshape(split_shape),
        preferred_element_type=jnp.float32,
    )
    result = result + jnp.einsum(
        "gts,bsgc->btgc",
        outer_part,
        before.reshape(split_shape),
        preferred_element_type=jnp.float32,
    )
    return result.reshape(blocks * length, feature_width)


def half_update(partial_value, block_keys, block_values, block_first, queries, positions):
    row_top, row_total, weighted = partial_value
    score_scale = HEAD_DIM ** (-0.5)
    scores = (
        jnp.einsum("qhd,khd->hqk", queries, block_keys, preferred_element_type=jnp.float32)
        * score_scale
    )
    key_positions = block_first + jnp.arange(block_keys.shape[0], dtype=jnp.int32)
    allowed = key_positions[None, :] <= positions[:, None]
    scores = jnp.where(allowed[None], scores, -jnp.inf)
    new_top = jnp.maximum(row_top, jnp.max(scores, axis=2))
    safe_top = jnp.where(new_top == -jnp.inf, 0.0, new_top)
    keep_factor = jnp.exp(row_top - safe_top)
    weights = jnp.exp(scores - safe_top[:, :, None])
    row_total = row_total * keep_factor + jnp.sum(weights, axis=2)
    weighted = weighted * keep_factor[:, :, None] + jnp.einsum(
        "hqk,khd->hqd",
        weights.astype(jnp.bfloat16),
        block_values,
        preferred_element_type=jnp.float32,
    )
    return (new_top, row_total, weighted)


def local(
    hyena_query,
    hyena_key,
    hyena_value,
    conv_filter,
    skip_gain,
    query_rows,
    key_rows,
    value_rows,
    out_weight,
):
    product = (hyena_key.astype(jnp.float32) * hyena_value.astype(jnp.float32)).astype(jnp.bfloat16)
    length = conv_filter.shape[1]
    tokens_here, feature_width = product.shape
    blocks = tokens_here // length
    previous = shifted(product[tokens_here - length :], "ctx", 1)
    widened = product.astype(jnp.float32)
    earlier = jnp.concatenate([previous, product[: tokens_here - length]], axis=0)
    convolved = local_conv(
        product.reshape(blocks, length, feature_width),
        earlier.reshape(blocks, length, feature_width),
        conv_filter,
    )
    hyena_out = (
        hyena_query.astype(jnp.float32) * (convolved + skip_gain[None, :] * widened)
    ).astype(jnp.bfloat16)
    ctx_index = lax.axis_index("ctx")
    half_rows = tokens_here // 2
    heads_here = feature_width // HEAD_DIM
    offsets = jnp.arange(half_rows, dtype=jnp.int32)
    first_positions = ctx_index * tokens_here + offsets
    second_queries = query_rows[half_rows:]
    second_positions = ctx_index * tokens_here + half_rows + offsets
    query_halves = (
        query_rows[:half_rows].reshape(half_rows, heads_here, HEAD_DIM),
        second_queries.reshape(half_rows, heads_here, HEAD_DIM),
    )
    position_halves = (first_positions, second_positions)
    empty_top = jnp.full((heads_here, half_rows), -jnp.inf, jnp.float32)
    empty_total = jnp.zeros((heads_here, half_rows), jnp.float32)
    empty_weighted = jnp.zeros((heads_here, half_rows, HEAD_DIM), jnp.float32)
    start_state = (
        (empty_top, empty_total, empty_weighted),
        (empty_top, empty_total, empty_weighted),
    )
    key_piece = lax.all_gather(key_rows, "ctx", axis=0, tiled=True)
    value_piece = lax.all_gather(value_rows, "ctx", axis=0, tiled=True)
    piece_rows = key_piece.shape[0]
    step_rows = min(piece_rows, tokens_here)
    count_steps = piece_rows // step_rows
    key_steps = key_piece.reshape(count_steps, step_rows, heads_here, HEAD_DIM)
    value_steps = value_piece.reshape(count_steps, step_rows, heads_here, HEAD_DIM)

    def one_step(carried, inputs):
        block_keys, block_values, step_index = inputs
        block_first = step_index * step_rows
        updated = []
        for half_index in range(2):
            queries = query_halves[half_index]
            positions = position_halves[half_index]

            def apply_update(partial_value, queries=queries, positions=positions):
                return half_update(
                    partial_value, block_keys, block_values, block_first, queries, positions
                )

            def leave_alone(partial_value):
                return partial_value

            updated.append(
                lax.cond(
                    block_first <= positions[half_rows - 1],
                    apply_update,
                    leave_alone,
                    carried[half_index],
                )
            )
        return ((updated[0], updated[1]), None)

    final_state, unused = lax.scan(
        one_step, start_state, (key_steps, value_steps, jnp.arange(count_steps, dtype=jnp.int32))
    )
    first_state, second_state = final_state

    def finish(partial_value):
        row_top, row_total, weighted = partial_value
        normalized = weighted / row_total[:, :, None]
        return (
            jnp.transpose(normalized, (1, 0, 2))
            .reshape(half_rows, feature_width)
            .astype(jnp.bfloat16)
        )

    first_result = finish(first_state)
    second_result = finish(second_state)
    attended = jnp.concatenate([first_result, second_result], axis=0)
    attention_out = lax.psum_scatter(
        lax.dot_general(
            out_weight, attended, (((1,), (1,)), ((), ())), preferred_element_type=jnp.float32
        ).astype(jnp.bfloat16),
        "tp",
        scatter_dimension=0,
        tiled=True,
    )
    return (hyena_out, attention_out)


def solution(mesh):
    in_specs = (
        P("ctx", "tp"),
        P("ctx", "tp"),
        P("ctx", "tp"),
        P("tp", None),
        P("tp"),
        P("ctx", "tp"),
        P("ctx", "tp"),
        P("ctx", "tp"),
        P(None, "tp"),
    )
    out_specs = (P("ctx", "tp"), P("tp", "ctx"))
    return jax.shard_map(local, mesh=mesh, in_specs=in_specs, out_specs=out_specs, check_vma=False)
```

profile of v0, /device:TPU:1, one launch (start us, length us, event | category | flops | bytes accessed | tf_op | source)
XLA Modules:
  0.0 493.8 jit_solution(8231100119584761282)
XLA Ops:
  8.7 1.2 slice_bitcast_fusion
  10.1 94.3 %all-gather.3.cloned.1.call-done = bf16[6144,1024]{1,0:T(8,128)(2,1)} async-done(((bf16[384,1024]{1,0:T(8,128)(2,1)}), bf16[6144,1024]{1,0:T(8,128)(2,1)}) %all-gather.3.cloned.1.call-update) | async-done | bytes 12582928 | tf_op jit(solution)/shard_map/all_gather | solution.py:121
  104.4 12.0 %copy.40 = bf16[768,8,8,128]{3,2,1,0:T(8,128)(2,1)} copy(bf16[768,8,8,128]{3,1,2,0:T(8,128)(2,1)} %bitcast.97) | data formatting | bytes 25165824
  116.4 78.6 %all-gather.5.cloned.1.call-done = bf16[6144,1024]{1,0:T(8,128)(2,1)} async-done(((bf16[384,1024]{1,0:T(8,128)(2,1)}), bf16[6144,1024]{1,0:T(8,128)(2,1)}) %all-gather.5.cloned.1.call-update) | async-done | bytes 12582928 | tf_op jit(solution)/shard_map/all_gather | solution.py:122
  195.0 11.9 %copy.41 = bf16[768,8,8,128]{3,2,1,0:T(8,128)(2,1)} copy(bf16[768,8,8,128]{3,1,2,0:T(8,128)(2,1)} %bitcast.98) | data formatting | bytes 25165824
  207.0 0.9 broadcast_in_dim.52
  207.9 103.0 %while.20 = (s32[]{:T(128)}, f32[8,192]{1,0:T(8,128)S(1)}, f32[8,192]{1,0:T(8,128)S(1)}, f32[8,192,128]{2,1,0:T(8,128)}, f32[8,192]{1,0:T(8,128)S(1)}, /*index=5...) while((s32[]{:T(128)}, f32[8,192]{1,0:T(8,128)S(1)}, ...), condition=%wide.region_9.10_spmd, body=%wide.region_0.9_spmd.sunk | while | flops 617908992 | bytes 34623508 | solution.py:155
  211.8 1.5 constant_dynamic-slice_fusion.3
  213.5 3.7 conditional.4
  214.3 0.9 fusion.2
  215.2 1.1 convolution_add_fusion
  217.2 2.8 conditional.5
  218.9 1.1 convolution_add_fusion.1
  223.8 1.5 constant_dynamic-slice_fusion.3
  225.6 3.7 conditional.4
  227.3 1.1 convolution_add_fusion
  229.3 2.8 conditional.5
  230.9 1.1 convolution_add_fusion.1
  235.9 1.5 constant_dynamic-slice_fusion.3
  241.6 1.5 constant_dynamic-slice_fusion.3
  247.2 1.5 constant_dynamic-slice_fusion.3
  252.8 1.5 constant_dynamic-slice_fusion.3
  258.5 1.5 constant_dynamic-slice_fusion.3
  264.1 1.5 constant_dynamic-slice_fusion.3
  269.7 1.5 constant_dynamic-slice_fusion.3
  275.4 1.5 constant_dynamic-slice_fusion.3
  281.0 1.5 constant_dynamic-slice_fusion.3
  286.6 1.5 constant_dynamic-slice_fusion.3
  292.3 1.5 constant_dynamic-slice_fusion.3
  297.9 1.5 constant_dynamic-slice_fusion.3
  303.5 1.5 constant_dynamic-slice_fusion.3
  309.2 1.5 constant_dynamic-slice_fusion.3
  311.2 1.4 copy_bitcast_fusion.3
  312.6 12.0 %fusion.20 = bf16[8192,384]{0,1:T(8,128)(2,1)} fusion(bf16[8192,1024]{1,0:T(8,128)(2,1)} %param.23, bf16[192,1024]{1,0:T(8,128)(2,1)S(1)} %copy_bitcast_fusion.2, bf16[192,1024]{1,0:T(8,128)(2,1)S(1)} %copy_bitcast_fusion.3), kind=kOutput, calls=%fused_computation.39 | convolution fusion | flops 6447169536 | bytes 23855104 | tf_op jit(solution)/shard_map/dot_general | solution.py:173
  324.7 1.1 copy-done.6
  326.8 9.1 %collective-permute-start = (bf16[128,1024]{0,1:T(8,128)(2,1)S(1)}, bf16[128,1024]{0,1:T(8,128)(2,1)}, u32[]{:S(2)}, u32[]{:S(2)}) collective-permute-start(bf16[128,1024]{0,1:T(8,128)(2,1)S(1)} %slice.22), channel_id=1, source_target_pairs={{0,8},{8,16},{16,24},{24,32},{32,40},{40,48},{48,56},{56,64},{64,7... | collective-permute-start | bytes 786440 | tf_op jit(solution)/shard_map/ppermute | solution.py:12
  336.2 1.1 copy.13
  337.3 1.2 iota_compare_fusion.1
  338.6 3.4 fusion.23
  342.0 2.3 fusion.26
  344.2 1.3 iota_compare_fusion
  345.5 4.7 fusion.21
  350.3 1.9 pad_maximum_fusion
  352.2 2.6 reshape_reshape.7
  354.8 4.0 add_bitcast_fusion
  360.5 1.2 copy.25
  361.7 123.3 %reduce-scatter.2.cloned.1.call-done = bf16[1024,384]{0,1:T(8,128)(2,1)} async-done(((bf16[8192,384]{0,1:T(8,128)(2,1)}), bf16[1024,384]{0,1:T(8,128)(2,1)}) %reduce-scatter.2.cloned.1.call-update) | async-done | bytes 786448 | tf_op jit(solution)/shard_map/reduce_scatter | solution.py:172
  485.0 2.3 copy.26
  (185 shorter events, 46.7 us)
Async XLA Ops:
  7.2 331.4 %copy-start = (bf16[64,128]{1,0:T(8,128)(2,1)S(1)}, bf16[64,128]{1,0:T(8,128)(2,1)}, u32[]{:S(2)}) copy-start(bf16[64,128]{1,0:T(8,128)(2,1)} %param.18) | copy-start | bytes 49156
  7.2 97.2 %all-gather.3.cloned.1.call-start = ((), (), s32[]{:S(2)}) async-start(), calls=%async_computation.1 | async-start | bytes 13369344 | tf_op jit(solution)/shard_map/all_gather | solution.py:121
  7.9 187.1 %all-gather.5.cloned.1.call-start = ((), (), s32[]{:S(2)}) async-start(), calls=%async_computation.2 | async-start | bytes 13369344 | tf_op jit(solution)/shard_map/all_gather | solution.py:122
  8.7 476.3 %reduce-scatter.2.cloned.1.call-start = ((), (), s32[]{:S(2)}) async-start(), calls=%async_computation.3 | async-start | bytes 7077888 | tf_op jit(solution)/shard_map/reduce_scatter | solution.py:172
  213.6 1.6 copy-start.4
  216.3 0.9 copy-start.5
  225.7 1.6 copy-start.4
  228.4 0.9 copy-start.5
  324.7 1.1 copy-start.6
  324.7 1.5 copy-start.7
  326.7 10.6 %copy-start.1 = (bf16[384,1024]{0,1:T(8,128)(2,1)}, bf16[384,1024]{0,1:T(8,128)(2,1)S(1)}, u32[]{:S(2)}) copy-start(bf16[384,1024]{0,1:T(8,128)(2,1)S(1)} %multiply_convert_fusion) | copy-start | bytes 2359300
  326.8 9.4 %copy-start.8 = (bf16[384,1024]{1,0:T(8,128)(2,1)S(1)}, bf16[384,1024]{1,0:T(8,128)(2,1)}, u32[]{:S(2)}) copy-start(bf16[384,1024]{1,0:T(8,128)(2,1)} %param.15) | copy-start | bytes 2359300
  326.8 23.5 %collective-permute-start = (bf16[128,1024]{0,1:T(8,128)(2,1)S(1)}, bf16[128,1024]{0,1:T(8,128)(2,1)}, u32[]{:S(2)}, u32[]{:S(2)}) collective-permute-start(bf16[128,1024]{0,1:T(8,128)(2,1)S(1)} %slice.22), channel_id=1, source_target_pairs={{0,8},{8,16},{16,24},{24,32},{32,40},{40,48},{48,56},{56,64},{64,7... | collective-permute-start | bytes 786440 | tf_op jit(solution)/shard_map/ppermute | solution.py:12
  345.5 4.7 slice-start
  358.8 1.1 copy-start.2
  358.8 1.4 copy-start.3
  358.8 1.4 copy-start.9
Sparse Core Ops, SparseCore 0:
  10.4 93.9 all-gather.2
  106.9 88.0 all-gather.4
  324.8 160.1 reduce-scatter.1
where the time goes:
time: 495 us; the launch traced here: 494 us
  waiting for transfers between devices  298 us (60%)
  local copies, waits for them, and re-layouts  96.2 us (19%)
  matrix products  33.3 us (7%)
  loops' own time  32.8 us (7%)
  between operations  14 us (3%)
  other arithmetic  10.8 us (2%)
  starting transfers between devices  9.21 us (2%)
    reduce_scatter x1, waiting for transfers between devices, local(): lax.psum_scatter(lax.dot_general(out_weight, attended, (((1,), (1,)), (()...  123 us
    all_gather x1, waiting for transfers between devices, local(): key_piece = lax.all_gather(key_rows, 'ctx', axis=0, tiled=True)  94.3 us
    all_gather x1, waiting for transfers between devices, local(): value_piece = lax.all_gather(value_rows, 'ctx', axis=0, tiled=True)  78.6 us
    dynamic_slice x64, local copies, waits for them, and re-layouts, local(): lax.scan(one_step, start_state, (key_steps, value_steps, jnp.arange(count...  37.4 us
    another operation x1, loops' own time, local(): lax.scan(one_step, start_state, (key_steps, value_steps, jnp.arange(count...  32 us
    unnamed x24, local copies, waits for them, and re-layouts  32 us
    slice x32, local copies, waits for them, and re-layouts, one_step(): positions[half_rows - 1]  20.1 us
    dot_general x1, matrix products, local(): lax.dot_general(out_weight, attended, (((1,), (1,)), ((), ())), preferred...  12 us
  transfers between devices with their start and end apart: 4, of which 3 were waited for; matrix products, arithmetic and copies ran while one was open for 8% of the time, Pallas kernels for 0%

commit v1 on v0

--- a/solution.py
+++ b/solution.py
@@ -118,7 +118,9 @@
         (empty_top, empty_total, empty_weighted),
         (empty_top, empty_total, empty_weighted),
     )
-    key_piece = lax.all_gather(key_rows, "ctx", axis=0, tiled=True)
+    key_piece = jnp.concatenate(
+        lax.all_to_all(jnp.stack([key_rows] * lax.axis_size("ctx")), "ctx", 0, 0), axis=0
+    )
     value_piece = lax.all_gather(value_rows, "ctx", axis=0, tiled=True)
     piece_rows = key_piece.shape[0]
     step_rows = min(piece_rows, tokens_here)

time: 495 us -> 537 us (1.085)
  waiting for transfers between devices: 298 us -> 322 us
  local copies, waits for them, and re-layouts: 96.2 us -> 108 us
  starting transfers between devices: 9.21 us -> 16.9 us
    all_gather x1, waiting for transfers between devices: 78.6 us -> 197 us  [local(): value_piece = lax.all_gather(value_rows, 'ctx', axis=0, tiled=True)]
    all_gather x1 -> x0, waiting for transfers between devices: 94.3 us -> none  [local(): key_piece = lax.all_gather(key_rows, 'ctx', axis=0, tiled=True)]
    dynamic_slice x64 -> x80, local copies, waits for them, and re-layouts: 37.4 us -> 56.1 us  [local(): lax.scan(one_step, start_state, (key_steps, value_steps, jnp.arange(count...]
    unnamed x24 -> x26, local copies, waits for them, and re-layouts: 32 us -> 20.4 us
    all_to_all x0 -> x1, starting transfers between devices: none -> 8.57 us  [local(): lax.all_to_all(jnp.stack([key_rows] * lax.axis_size('ctx')), 'ctx', 0, 0)]
    another operation x2 -> x3, local copies, waits for them, and re-layouts: 0.01 us -> 6.1 us  [the longest x1 6.09 us: local(): jnp.stack([key_rows] * lax.axis_size('ctx'))]
  transfers between devices with their start and end apart: 4 -> 4, of which waited for: 3 -> 2; matrix products, arithmetic and copies ran while one was open for 8% -> 9% of each run, Pallas kernels for 0% -> 0%
where the time goes in v1:
time: 537 us; the launch traced here: 535 us
  waiting for transfers between devices  322 us (60%)
  local copies, waits for them, and re-layouts  108 us (20%)
  matrix products  33.2 us (6%)
  loops' own time  29.8 us (6%)
  starting transfers between devices  16.9 us (3%)
  between operations  14.3 us (3%)
  other arithmetic  10.8 us (2%)
    all_gather x1, waiting for transfers between devices, local(): value_piece = lax.all_gather(value_rows, 'ctx', axis=0, tiled=True)  197 us
    reduce_scatter x1, waiting for transfers between devices, local(): lax.psum_scatter(lax.dot_general(out_weight, attended, (((1,), (1,)), (()...  123 us
    dynamic_slice x80, local copies, waits for them, and re-layouts, local(): lax.scan(one_step, start_state, (key_steps, value_steps, jnp.arange(count...  56.1 us
    another operation x1, loops' own time, local(): lax.scan(one_step, start_state, (key_steps, value_steps, jnp.arange(count...  29.1 us
    unnamed x26, local copies, waits for them, and re-layouts  20.4 us
    slice x32, local copies, waits for them, and re-layouts, one_step(): positions[half_rows - 1]  18.4 us
    dot_general x1, matrix products, local(): lax.dot_general(out_weight, attended, (((1,), (1,)), ((), ())), preferred...  12 us
  transfers between devices with their start and end apart: 4, of which 2 were waited for; matrix products, arithmetic and copies ran while one was open for 9% of the time, Pallas kernels for 0%

profile of v1, /device:TPU:1, one launch (start us, length us, event | category | flops | bytes accessed | tf_op | source)
XLA Modules:
  0.0 535.0 jit_solution(17096273900083676755)
XLA Ops:
  7.9 1.5 copy.19
  9.4 6.1 %stack.2 = bf16[16,384,1024]{1,2,0:T(8,128)(2,1)} broadcast(bf16[384,1024]{0,1:T(8,128)(2,1)S(1)} %copy.19), dimensions={1,2} | broadcast | bytes 13369344 | tf_op jit(solution)/shard_map/stack | solution.py:122
  15.5 8.6 %all-to-all-start = ((bf16[16,384,1024]{1,2,0:T(8,128)(2,1)}), bf16[16,384,1024]{1,2,0:T(8,128)(2,1)}, u32[]{:S(2)}, u32[]{:S(2)}) async-start(bf16[16,384,1024]{1,2,0:T(8,128)(2,1)} %stack.2), calls=%async_computation | async-start | bytes 25165824 | tf_op jit(solution)/shard_map/all_to_all | solution.py:122
  24.4 197.5 %all-gather.2.cloned.1.call-done = bf16[6144,1024]{1,0:T(8,128)(2,1)} async-done(((bf16[384,1024]{1,0:T(8,128)(2,1)}), bf16[6144,1024]{1,0:T(8,128)(2,1)}) %all-gather.2.cloned.1.call-update) | async-done | bytes 12582928 | tf_op jit(solution)/shard_map/all_gather | solution.py:124
  221.8 11.9 %copy.41 = bf16[768,8,8,128]{3,2,1,0:T(8,128)(2,1)} copy(bf16[768,8,8,128]{3,1,2,0:T(8,128)(2,1)} %bitcast.92) | data formatting | bytes 25165824
  234.8 117.0 %while.20 = (s32[]{:T(128)}, f32[8,192]{1,0:T(8,128)S(1)}, f32[8,192]{1,0:T(8,128)S(1)}, f32[8,192,128]{2,1,0:T(8,128)S(1)}, f32[8,192]{1,0:T(8,128)S(1)}, /*ind...) while((s32[]{:T(128)}, f32[8,192]{1,0:T(8,128)S(1)}, ...), condition=%wide.region_9.10_spmd, body=%wide.region_0.9_spmd.sunk | while | flops 617908992 | bytes 34623504 | solution.py:157
  236.0 1.2 constant_dynamic-slice_fusion.4
  240.1 3.7 conditional.5
  244.9 2.8 conditional.4
  249.0 1.2 constant_dynamic-slice_fusion.4
  253.1 3.7 conditional.5
  257.9 2.8 conditional.4
  262.0 1.2 constant_dynamic-slice_fusion.4
  263.6 1.2 constant_dynamic-slice_fusion.5
  268.5 1.2 constant_dynamic-slice_fusion.4
  270.1 1.2 constant_dynamic-slice_fusion.5
  275.0 1.2 constant_dynamic-slice_fusion.4
  281.5 1.2 constant_dynamic-slice_fusion.4
  288.0 1.2 constant_dynamic-slice_fusion.4
  289.6 1.2 constant_dynamic-slice_fusion.5
  294.5 1.2 constant_dynamic-slice_fusion.4
  296.1 1.2 constant_dynamic-slice_fusion.5
  301.0 1.2 constant_dynamic-slice_fusion.4
  302.6 1.2 constant_dynamic-slice_fusion.5
  307.5 1.2 constant_dynamic-slice_fusion.4
  314.0 1.2 constant_dynamic-slice_fusion.4
  315.6 1.2 constant_dynamic-slice_fusion.5
  320.5 1.2 constant_dynamic-slice_fusion.4
  322.1 1.2 constant_dynamic-slice_fusion.5
  327.0 1.2 constant_dynamic-slice_fusion.4
  328.6 1.2 constant_dynamic-slice_fusion.5
  333.5 1.2 constant_dynamic-slice_fusion.4
  340.0 1.2 constant_dynamic-slice_fusion.4
  346.5 1.2 constant_dynamic-slice_fusion.4
  348.1 1.2 constant_dynamic-slice_fusion.5
  352.1 1.4 copy_bitcast_fusion.1
  353.5 12.0 %fusion.20 = bf16[8192,384]{0,1:T(8,128)(2,1)} fusion(bf16[8192,1024]{1,0:T(8,128)(2,1)} %param.23, bf16[192,1024]{1,0:T(8,128)(2,1)S(1)} %copy_bitcast_fusion.1, bf16[192,1024]{1,0:T(8,128)(2,1)S(1)} %copy_bitcast_fusion.2), kind=kOutput, calls=%fused_computation.38 | convolution fusion | flops 6447169536 | bytes 23855104 | tf_op jit(solution)/shard_map/dot_general | solution.py:175
  368.3 8.3 %collective-permute-start = (bf16[128,1024]{0,1:T(8,128)(2,1)}, bf16[128,1024]{0,1:T(8,128)(2,1)}, u32[]{:S(2)}, u32[]{:S(2)}) collective-permute-start(bf16[128,1024]{0,1:T(8,128)(2,1)} %slice.22), channel_id=1, source_target_pairs={{0,8},{8,16},{16,24},{24,32},{32,40},{40,48},{48,56},{56,64},{64,7... | collective-permute-start | bytes 786440 | tf_op jit(solution)/shard_map/ppermute | solution.py:12
  378.0 1.2 iota_compare_fusion.1
  379.3 3.4 fusion.23
  382.6 2.3 fusion.26
  384.9 1.3 iota_compare_fusion
  386.2 4.7 fusion.21
  390.9 1.9 pad_maximum_fusion
  392.8 2.6 reshape_reshape.10
  395.5 4.0 add_bitcast_fusion
  402.4 123.5 %reduce-scatter.2.cloned.1.call-done = bf16[1024,384]{0,1:T(8,128)(2,1)} async-done(((bf16[8192,384]{0,1:T(8,128)(2,1)}), bf16[1024,384]{0,1:T(8,128)(2,1)}) %reduce-scatter.2.cloned.1.call-update) | async-done | bytes 786448 | tf_op jit(solution)/shard_map/reduce_scatter | solution.py:174
  525.9 2.3 copy.27
  (203 shorter events, 66.7 us)
Async XLA Ops:
  7.2 372.1 %copy-start = (bf16[64,128]{1,0:T(8,128)(2,1)S(1)}, bf16[64,128]{1,0:T(8,128)(2,1)}, u32[]{:S(2)}) copy-start(bf16[64,128]{1,0:T(8,128)(2,1)} %param.18) | copy-start | bytes 49156
  7.2 214.7 %all-gather.2.cloned.1.call-start = ((), (), s32[]{:S(2)}) async-start(), calls=%async_computation.2 | async-start | bytes 13369344 | tf_op jit(solution)/shard_map/all_gather | solution.py:124
  15.5 8.6 %copy-start.6 = (bf16[384,1024]{1,0:T(8,128)(2,1)S(1)}, bf16[384,1024]{1,0:T(8,128)(2,1)}, u32[]{:S(2)}) copy-start(bf16[384,1024]{1,0:T(8,128)(2,1)} %param.20) | copy-start | bytes 2359300
  15.5 218.2 %all-to-all-start = ((bf16[16,384,1024]{1,2,0:T(8,128)(2,1)}), bf16[16,384,1024]{1,2,0:T(8,128)(2,1)}, u32[]{:S(2)}, u32[]{:S(2)}) async-start(bf16[16,384,1024]{1,2,0:T(8,128)(2,1)} %stack.2), calls=%async_computation | async-start | bytes 25165824 | tf_op jit(solution)/shard_map/all_to_all | solution.py:122
  24.1 501.8 %reduce-scatter.2.cloned.1.call-start = ((), (), s32[]{:S(2)}) async-start(), calls=%async_computation.3 | async-start | bytes 7077888 | tf_op jit(solution)/shard_map/reduce_scatter | solution.py:174
  240.2 1.6 copy-start.4
  242.9 0.9 copy-start.5
  253.2 1.6 copy-start.4
  255.9 0.9 copy-start.5
  365.4 1.1 copy-start.7
  365.4 1.5 copy-start.8
  367.5 10.5 %copy-start.1 = (bf16[384,1024]{0,1:T(8,128)(2,1)}, bf16[384,1024]{0,1:T(8,128)(2,1)S(1)}, u32[]{:S(2)}) copy-start(bf16[384,1024]{0,1:T(8,128)(2,1)S(1)} %multiply_convert_fusion) | copy-start | bytes 2359300
  367.5 9.3 %copy-start.9 = (bf16[384,1024]{1,0:T(8,128)(2,1)S(1)}, bf16[384,1024]{1,0:T(8,128)(2,1)}, u32[]{:S(2)}) copy-start(bf16[384,1024]{1,0:T(8,128)(2,1)} %param.15) | copy-start | bytes 2359300
  368.3 22.7 %collective-permute-start = (bf16[128,1024]{0,1:T(8,128)(2,1)}, bf16[128,1024]{0,1:T(8,128)(2,1)}, u32[]{:S(2)}, u32[]{:S(2)}) collective-permute-start(bf16[128,1024]{0,1:T(8,128)(2,1)} %slice.22), channel_id=1, source_target_pairs={{0,8},{8,16},{16,24},{24,32},{32,40},{40,48},{48,56},{56,64},{64,7... | collective-permute-start | bytes 786440 | tf_op jit(solution)/shard_map/ppermute | solution.py:12
  386.2 4.8 slice-start
  399.4 1.1 copy-start.2
  399.5 1.4 copy-start.3
  399.5 1.4 copy-start.10
Sparse Core Ops, SparseCore 0:
  10.4 211.3 all-gather.1
  365.6 160.2 reduce-scatter.1
